TPU v7x, 256 devices: a whole 4x4x8 slice. The times are simulated.
256 devices in a mesh: blk: 8 (over y, core), wide: 32 (over x, z).
Axes of the slice: x: 4, y: 4, z: 8, core: 2. Of those that a mesh axis runs over, the one named last changes fastest.
Arguments:
- amplitudes: bfloat16 [2048, 262144], P(('blk', 'wide')), may hold values from -6 to 6
- integrals: bfloat16 [32, 256, 128, 128], P('wide', 'blk'), may hold values from -0.03125 to 0.03125
- out_tile: int32 [32, 256], P('wide'), may hold values from 0 to 31, as said below
- cd_slot: int32 [32, 256], P('wide'), may hold values from 0 to 63, as said below
Outputs:
- ladder: bfloat16 [2048, 4096], P('blk', 'wide')
Inputs may be any that keep to these rules, and one draw needn't show every extreme that they name: `out_tile`: output tile a lies in sector a mod 8. In each group every one of its 64 contracted tiles appears in exactly 4 entries, once with each output tile of one sector, the sector drawn for that tile; entries are in no particular order. `cd_slot`: see out_tile.
All inputs are finite; a program needn't handle non-finite values.
Results may differ from a plain program's by a relative error of at most 0.001.
Values may be sent and summed in bfloat16 or wider, within the bound.
No kernel may reach another device: no remote copies, remote signals or barrier semaphores. Data moves between devices by JAX's collectives and lax.ppermute only.
A program may use at most 192 MiB of HBM per device.

v0:
```python
import jax
import jax.numpy as jnp
from jax import lax
from jax.experimental import pallas as pl
from jax.experimental.pallas import tpu as pltpu
from jax.sharding import Mesh
from jax.sharding import PartitionSpec as P

SECTORS = 8
A_PER = 4
TILE = 128
SLOTS = 64
ENTRIES = SLOTS * A_PER
PAIRS = (SLOTS + SECTORS) // 2
PAD_SLOTS = 2 * PAIRS
ROWS = 256
CODE_ROWS = ROWS + 16
STEP_PAIRS = 4
STEPS = PAIRS // STEP_PAIRS
TOP = 32760.0
TINY = 1e-30
GRAIN = 64.0


def tables(out_tile, cd_slot, y, c):
    entry = jnp.arange(ENTRIES, dtype=jnp.int32)
    key = cd_slot * A_PER + out_tile // SECTORS
    hit = key[None, :] == entry[:, None]
    where_entry = jnp.sum(jnp.where(hit, entry[None, :], 0), axis=1)
    source = where_entry // (ENTRIES // 8)
    hop = (y - source // 2) % 4
    other = jnp.where(source % 2 == c, 0, 1)
    place = ((other * 4 + hop) * (ENTRIES // 8) + where_entry % (ENTRIES // 8)).reshape(SLOTS, A_PER)
    sector = jnp.sum(jnp.where(hit, out_tile[None, :] % SECTORS, 0), axis=1).reshape(SLOTS, A_PER)[:, 0]
    slot = jnp.arange(SLOTS, dtype=jnp.int32)
    of_sector = sector[None, :] == jnp.arange(SECTORS, dtype=jnp.int32)[:, None]
    padded = (jnp.sum(of_sector.astype(jnp.int32), axis=1) + 1) // 2 * 2
    before = jnp.arange(SECTORS)[None, :] < jnp.arange(SECTORS)[:, None]
    start = jnp.sum(jnp.where(before, padded[None, :], 0), axis=1)
    earlier = (sector[None, :] == sector[:, None]) & (slot[None, :] < slot[:, None])
    rank = jnp.sum(earlier.astype(jnp.int32), axis=1)
    position = jnp.sum(jnp.where(of_sector, start[:, None], 0), axis=0) + rank
    at = position[None, :] == jnp.arange(PAD_SLOTS, dtype=jnp.int32)[:, None]
    valid = jnp.sum(at.astype(jnp.int32), axis=1)
    order = jnp.sum(jnp.where(at, slot[None, :], 0), axis=1)
    order_place = jnp.sum(jnp.where(at[:, :, None], place[None, :, :], 0), axis=1)
    pair_first = 2 * jnp.arange(PAIRS, dtype=jnp.int32)
    pair_sector = jnp.sum((start[None, :] <= pair_first[:, None]).astype(jnp.int32), axis=1) - 1
    return order, valid, order_place.reshape(-1), pair_sector


def arrange_kernel(valid, place, same_core, other_core, out, held, sem):
    j = pl.program_id(0)

    @pl.when(j == 0)
    def _():
        half = ENTRIES // 2
        one = pltpu.make_async_copy(same_core, held.at[:half], sem.at[0])
        two = pltpu.make_async_copy(other_core, held.at[half:], sem.at[1])
        one.start()
        two.start()
        one.wait()
        two.wait()

    for i in range(2 * STEP_PAIRS):
        at = j * 2 * STEP_PAIRS + i

        @pl.when(valid[at] == 1)
        def _():
            for r in range(A_PER):
                out[i, :, r * TILE : (r + 1) * TILE] = held[place[at * A_PER + r]]

        @pl.when(valid[at] == 0)
        def _():
            out[i] = jnp.zeros((TILE, A_PER * TILE), out.dtype)


def arrange(valid, place, same_core, other_core):
    return pl.pallas_call(
        arrange_kernel,
        grid_spec=pltpu.PrefetchScalarGridSpec(
            num_scalar_prefetch=2,
            grid=(STEPS,),
            in_specs=[pl.BlockSpec(memory_space=pl.ANY)] * 2,
            out_specs=pl.BlockSpec((2 * STEP_PAIRS, TILE, A_PER * TILE), lambda j, v, p: (j, 0, 0)),
            scratch_shapes=[
                pltpu.VMEM((ENTRIES, TILE, TILE), jnp.bfloat16),
                pltpu.SemaphoreType.DMA((2,)),
            ],
        ),
        out_shape=jax.ShapeDtypeStruct((PAD_SLOTS, TILE, A_PER * TILE), jnp.bfloat16),
        cost_estimate=pl.CostEstimate(flops=0, bytes_accessed=2 * 9 * 2**20, transcendentals=0),
        name="arrange",
    )(valid, place, same_core, other_core)


def put_codes(out, v):
    top = jnp.maximum(jnp.max(jnp.abs(v), axis=0, keepdims=True), TINY)
    level = jnp.ceil(jnp.log2(top) * GRAIN + 1.0)
    factor = TOP * jnp.exp2(-level * (1.0 / GRAIN))
    out[:ROWS, :] = jnp.round(v * factor).astype(jnp.int32).astype(jnp.int16)
    out[ROWS:, :] = jnp.broadcast_to(level.astype(jnp.int32), (CODE_ROWS - ROWS, TILE)).astype(jnp.int16)


def get_codes(codes):
    level = codes[ROWS:, :].astype(jnp.int32).astype(jnp.float32)[:1]
    scale = jnp.exp2(level * (1.0 / GRAIN)) * (1.0 / TOP)
    return codes[:ROWS, :].astype(jnp.int32).astype(jnp.float32) * scale


def ladder_kernel(order, pair_sector, *refs):
    tiles, (w, out, acc) = refs[: 2 * STEP_PAIRS], refs[2 * STEP_PAIRS :]
    step = pl.program_id(0)

    @pl.when(step == 0)
    def _():
        acc[...] = jnp.zeros_like(acc)

    for i in range(STEP_PAIRS):
        s = pair_sector[step * STEP_PAIRS + i]
        left = jnp.concatenate([tiles[2 * i][...], tiles[2 * i + 1][...]], axis=1)
        right = w[2 * i : 2 * i + 2].reshape(2 * TILE, A_PER * TILE)
        acc[s] += jnp.dot(left, right, preferred_element_type=jnp.float32)

    @pl.when(step == STEPS - 1)
    def _():
        def encode(s, _):
            for r in range(A_PER):
                put_codes(out.at[r, s], acc[s, :, r * TILE : (r + 1) * TILE])
            return 0

        lax.fori_loop(0, SECTORS, encode, 0)


def ladder_codes(order, pair_sector, x, w):
    def tile(i):
        return pl.BlockSpec((ROWS, TILE), lambda j, o, p: (0, o[j * 2 * STEP_PAIRS + i]))

    return pl.pallas_call(
        ladder_kernel,
        grid_spec=pltpu.PrefetchScalarGridSpec(
            num_scalar_prefetch=2,
            grid=(STEPS,),
            in_specs=[tile(i) for i in range(2 * STEP_PAIRS)]
            + [pl.BlockSpec((2 * STEP_PAIRS, TILE, A_PER * TILE), lambda j, o, p: (j, 0, 0))],
            out_specs=pl.BlockSpec((A_PER, SECTORS, CODE_ROWS, TILE), lambda j, o, p: (0, 0, 0, 0)),
            scratch_shapes=[pltpu.VMEM((SECTORS, ROWS, A_PER * TILE), jnp.float32)],
        ),
        out_shape=jax.ShapeDtypeStruct((A_PER, SECTORS, CODE_ROWS, TILE), jnp.int16),
        cost_estimate=pl.CostEstimate(flops=2 * 36 * 256 * 256 * 512, bytes_accessed=16 * 2**20, transcendentals=0),
        name="ladder_codes",
    )(order, pair_sector, *[x] * (2 * STEP_PAIRS), w)


def recode_kernel(codes, out):
    put_codes(out.at[0], sum(get_codes(codes.at[i, 0]) for i in range(A_PER)))


def recode(codes):
    return pl.pallas_call(
        recode_kernel,
        grid=(SECTORS,),
        in_specs=[pl.BlockSpec((A_PER, 1, CODE_ROWS, TILE), lambda j: (0, j, 0, 0))],
        out_specs=pl.BlockSpec((1, CODE_ROWS, TILE), lambda j: (j, 0, 0)),
        out_shape=jax.ShapeDtypeStruct((SECTORS, CODE_ROWS, TILE), jnp.int16),
        name="recode",
    )(codes)


def total_kernel(codes, out):
    out[...] = sum(get_codes(codes.at[i]) for i in range(SECTORS)).astype(jnp.bfloat16)


def total(codes):
    return pl.pallas_call(total_kernel, out_shape=jax.ShapeDtypeStruct((ROWS, TILE), jnp.bfloat16), name="total")(codes)


def on_device(amplitudes, integrals, out_tile, cd_slot):
    y, c = lax.axis_index("y"), lax.axis_index("c")
    order, valid, place, pair_sector = tables(out_tile[0], cd_slot[0], y, c)
    mine = integrals[0]
    same_core = [mine] + [lax.ppermute(mine, "y", [(i, (i + d) % 4) for i in range(4)]) for d in (1, 2, 3)]
    same_core = jnp.concatenate(same_core, axis=0)
    other_core = lax.ppermute(same_core, "c", [(0, 1), (1, 0)])
    w = arrange(valid, place, same_core, other_core)
    exchanged = lax.all_to_all(amplitudes, ("x", "z"), split_axis=1, concat_axis=0, tiled=True)
    codes = ladder_codes(order, pair_sector, exchanged, w)
    codes = lax.all_to_all(codes, "x", split_axis=0, concat_axis=0, tiled=True)
    codes = lax.all_to_all(recode(codes), "z", split_axis=0, concat_axis=0, tiled=True)
    return total(codes)


def solution(mesh):
    grid = Mesh(mesh.devices.reshape(4, 2, 4, 8), ("y", "c", "x", "z"))
    blk, wide = ("y", "c"), ("x", "z")
    in_specs = (P(blk + wide, None), P(wide, blk, None, None), P(wide, None), P(wide, None))
    return jax.shard_map(on_device, mesh=grid, in_specs=in_specs, out_specs=P(blk, wide), check_vma=False)
```

profile of v0, /device:TPU:16, one launch (start us, length us, event | category | flops | bytes accessed | tf_op | source)
XLA Modules:
  0.0 181.3 jit_solution(9185934033517153585)
XLA Ops:
  0.0 0.0 copy-start
  0.0 11.6 %all-to-all-start = ((bf16[8,32,8192]{2,0,1:T(8,128)(2,1)}), bf16[8,32,8192]{2,0,1:T(8,128)(2,1)}, u32[]{:S(2)}, u32[]{:S(2)}) async-start(bf16[8,32,8192]{2,0,1:T(8,128)(2,1)} %bitcast.7), calls=%async_computation | async-start | bytes 8388608 | tf_op jit(solution)/shard_map/all_to_all | solution.py:186
  11.6 0.0 copy-done
  11.6 0.0 copy-start.1
  11.6 0.0 copy-start.2
  11.6 1.4 collective-permute-start
  13.0 0.6 collective-permute-start.1
  13.6 1.1 collective-permute-start.2
  14.7 44.1 %collective-permute-done = bf16[32,128,128]{2,1,0:T(8,128)(2,1)S(1)} collective-permute-done((bf16[32,128,128]{2,1,0:T(8,128)(2,1)S(1)}, bf16[32,128,128]{2,1,0:T(8,128)(2,1)S(1)}, u32[]{:S(2)}, u32[]{:S(2)}) %collective-permute-start) | collective-permute-done | bytes 1048608 | tf_op jit(solution)/shard_map/ppermute | solution.py:182
  58.8 0.0 collective-permute-done.1
  58.8 1.8 %collective-permute-done.2 = bf16[32,128,128]{2,1,0:T(8,128)(2,1)S(1)} collective-permute-done((bf16[32,128,128]{2,1,0:T(8,128)(2,1)S(1)}, bf16[32,128,128]{2,1,0:T(8,128)(2,1)S(1)}, u32[]{:S(2)}, u32[]{:S(2)}) %collective-permute-start.2) | collective-permute-done | bytes 1048608 | tf_op jit(solution)/shard_map/ppermute | solution.py:182
  60.6 2.2 %pad_maximum_fusion.same_core = bf16[128,128,128]{2,1,0:T(8,128)(2,1)} fusion(bf16[32,128,128]{2,1,0:T(8,128)(2,1)S(1)} %collective-permute-done.2, bf16[32,128,128]{2,1,0:T(8,128)(2,1)S(1)} %collective-permute-done.1, bf16[32,128,128]{2,1,0:T(8,128)(2,1)S(1)} %collective-permute-done, bf16[32,128,128]{2,1,0:T(8,128)(2,1)S(1)} %bitcast.11), kind=kLoop, calls=%fused_computation | loop fusion | flops 6291456 | bytes 8388608 | tf_op jit(solution)/shard_map/concatenate | solution.py:183
  62.9 0.0 collective-permute-start.3
  62.9 0.0 copy-done.1
  62.9 0.0 copy-done.2
  62.9 0.2 select_reduce_fusion
  63.1 0.1 reshape.151
  63.2 0.1 reduce_sum.101
  63.3 0.1 fusion.5
  63.4 0.1 copy.5
  63.5 0.1 slice_reduce_fusion
  63.6 0.1 convert_reduce_fusion.3
  63.7 0.1 select_reduce_fusion.5
  63.8 0.2 convert_reduce_fusion.1
  64.0 0.1 select_reduce_fusion.4
  64.1 0.1 iota_compare_fusion.1
  64.2 0.1 select_reduce_fusion.2
  64.3 0.1 copy.6
  64.4 0.7 reshape.152.place
  65.1 0.7 convert_reduce_fusion
  65.8 0.1 convert_reduce_fusion.2
  65.9 0.5 broadcast_add_fusion.pair_sector
  66.4 4.0 %collective-permute-done.3.other_core = bf16[128,128,128]{2,1,0:T(8,128)(2,1)} collective-permute-done((bf16[128,128,128]{2,1,0:T(8,128)(2,1)}, bf16[128,128,128]{2,1,0:T(8,128)(2,1)}, u32[]{:S(2)}, u32[]{:S(2)}) %collective-permute-start.3) | collective-permute-done | bytes 4194336 | tf_op jit(solution)/shard_map/ppermute | solution.py:184
  70.4 10.6 %arrange.1.refs_8_ = bf16[72,128,512]{2,1,0:T(8,128)(2,1)} custom-call(s32[72]{0:T(128)} %get-tuple-element.7.valid, s32[288]{0:T(512)} %reshape.152.place, bf16[128,128,128]{2,1,0:T(8,128)(2,1)} %pad_maximum_fusion.same_core, bf16[128,128,128]{2,1,0:T(8,128)(2,1)} %collective-permute-done.3.other_core), custom_call_target="tpu_custom_call" | custom-call | bytes 18874368 | tf_op jit(solution)/shard_map/arrange/pallas_call | solution.py:79
  81.0 27.6 %all-to-all-done = bf16[8,32,8192]{2,0,1:T(8,128)(2,1)} async-done(((bf16[8,32,8192]{2,0,1:T(8,128)(2,1)}), bf16[8,32,8192]{2,0,1:T(8,128)(2,1)}, u32[]{:S(2)}, u32[]{:S(2)}) %all-to-all-start) | async-done | bytes 4194336 | tf_op jit(solution)/shard_map/all_to_all | solution.py:186
  108.6 12.9 %ladder_codes.1 = s16[4,8,272,128]{3,2,1,0:T(8,128)(2,1)} custom-call(s32[72]{0:T(128)} %get-tuple-element.8.order, s32[36]{0:T(128)} %broadcast_add_fusion.pair_sector, bf16[256,8192]{1,0:T(8,128)(2,1)} %bitcast.4.refs_0_.refs_1_.refs_2_.refs_3_.refs_4_.refs_5_.refs_6_.refs_7_, ...), custom_call_target="tpu_custom_call" | custom-call | flops 2415919104 | bytes 16777216 | tf_op jit(solution)/shard_map/ladder_codes/pallas_call | solution.py:139
  121.5 27.7 %all_to_all.29.codes = s16[4,8,272,128]{3,2,1,0:T(8,128)(2,1)} all-to-all(s16[4,8,272,128]{3,2,1,0:T(8,128)(2,1)} %ladder_codes.1), channel_id=1, replica_groups=mesh['y'=4,'c'=2,'x'=4,'z'=8] {'x'}, dimensions={0} | all-to-all | bytes 4456448 | tf_op jit(solution)/shard_map/all_to_all | solution.py:188
  149.2 5.7 %recode.1 = s16[8,272,128]{2,1,0:T(8,128)(2,1)} custom-call(s16[4,8,272,128]{3,2,1,0:T(8,128)(2,1)} %all_to_all.29.codes), custom_call_target="tpu_custom_call" | custom-call | tf_op jit(solution)/shard_map/recode/pallas_call | solution.py:160
  154.9 24.6 %all_to_all.30.codes = s16[8,272,128]{2,1,0:T(8,128)(2,1)} all-to-all(s16[8,272,128]{2,1,0:T(8,128)(2,1)} %recode.1), channel_id=1, replica_groups=mesh['y'=4,'c'=2,'x'=4,'z'=8] {'z'}, dimensions={0} | all-to-all | bytes 1114112 | tf_op jit(solution)/shard_map/all_to_all | solution.py:189
  179.5 1.8 %total.1 = bf16[256,128]{1,0:T(8,128)(2,1)} custom-call(s16[8,272,128]{2,1,0:T(8,128)(2,1)} %all_to_all.30.codes), custom_call_target="tpu_custom_call" | custom-call | tf_op jit(solution)/shard_map/total/pallas_call | solution.py:175
  (4 shorter events, 0.0 us)
Async XLA Ops:
  0.0 11.6 %copy-start = (bf16[1,32,128,128]{3,2,1,0:T(8,128)(2,1)S(1)}, bf16[1,32,128,128]{3,2,1,0:T(8,128)(2,1)}, u32[]{:S(2)}) copy-start(bf16[1,32,128,128]{3,2,1,0:T(8,128)(2,1)} %param.5) | copy-start | bytes 3145732
  0.0 108.6 %all-to-all-start = ((bf16[8,32,8192]{2,0,1:T(8,128)(2,1)}), bf16[8,32,8192]{2,0,1:T(8,128)(2,1)}, u32[]{:S(2)}, u32[]{:S(2)}) async-start(bf16[8,32,8192]{2,0,1:T(8,128)(2,1)} %bitcast.7), calls=%async_computation | async-start | bytes 8388608 | tf_op jit(solution)/shard_map/all_to_all | solution.py:186
  11.6 51.3 %copy-start.1 = (s32[1,256]{1,0:T(1,128)S(1)}, s32[1,256]{1,0:T(1,128)}, u32[]{:S(2)}) copy-start(s32[1,256]{1,0:T(1,128)} %param.6) | copy-start | bytes 3076
  11.6 51.3 %copy-start.2 = (s32[1,256]{1,0:T(1,128)S(1)}, s32[1,256]{1,0:T(1,128)}, u32[]{:S(2)}) copy-start(s32[1,256]{1,0:T(1,128)} %param.7) | copy-start | bytes 3076
  11.6 47.2 %collective-permute-start = (bf16[32,128,128]{2,1,0:T(8,128)(2,1)S(1)}, bf16[32,128,128]{2,1,0:T(8,128)(2,1)S(1)}, u32[]{:S(2)}, u32[]{:S(2)}) collective-permute-start(bf16[32,128,128]{2,1,0:T(8,128)(2,1)S(1)} %bitcast.8), channel_id=1, source_target_pairs={{0,64},{64,128},{128,192},{192,0},{1,65},{65,129},{129,193},{193,1... | collective-permute-start | bytes 3145736 | tf_op jit(solution)/shard_map/ppermute | solution.py:182
  13.0 45.8 %collective-permute-start.1 = (bf16[32,128,128]{2,1,0:T(8,128)(2,1)S(1)}, bf16[32,128,128]{2,1,0:T(8,128)(2,1)S(1)}, u32[]{:S(2)}, u32[]{:S(2)}) collective-permute-start(bf16[32,128,128]{2,1,0:T(8,128)(2,1)S(1)} %bitcast.9), channel_id=1, source_target_pairs={{0,128},{64,192},{128,0},{192,64},{1,129},{65,193},{129,1},{193,65... | collective-permute-start | bytes 3145736 | tf_op jit(solution)/shard_map/ppermute | solution.py:182
  13.6 47.0 %collective-permute-start.2 = (bf16[32,128,128]{2,1,0:T(8,128)(2,1)S(1)}, bf16[32,128,128]{2,1,0:T(8,128)(2,1)S(1)}, u32[]{:S(2)}, u32[]{:S(2)}) collective-permute-start(bf16[32,128,128]{2,1,0:T(8,128)(2,1)S(1)} %bitcast.10), channel_id=1, source_target_pairs={{0,192},{64,0},{128,64},{192,128},{1,193},{65,1},{129,65},{193,129... | collective-permute-start | bytes 3145736 | tf_op jit(solution)/shard_map/ppermute | solution.py:182
  62.9 7.5 %collective-permute-start.3 = (bf16[128,128,128]{2,1,0:T(8,128)(2,1)}, bf16[128,128,128]{2,1,0:T(8,128)(2,1)}, u32[]{:S(2)}, u32[]{:S(2)}) collective-permute-start(bf16[128,128,128]{2,1,0:T(8,128)(2,1)} %pad_maximum_fusion.same_core), channel_id=1, source_target_pairs={{0,32},{32,0},{1,33},{33,1},{2,34},{34,2},{3,35},{35,3},{4,36},{36... | collective-permute-start | bytes 12582920 | tf_op jit(solution)/shard_map/ppermute | solution.py:184
where the time goes:
time: 182 us; the launch traced here: 181 us
  waiting for transfers between devices  77.5 us (43%)
  blocking collectives  52.3 us (29%)
  Pallas kernels  31 us (17%)
  starting transfers between devices  14.6 us (8%)
  other arithmetic  4.51 us (2%)
    ppermute x3, waiting for transfers between devices, on_device(): lax.ppermute(mine, 'y', [(i, (i + d) % 4) for i in range(4)])  46 us
    all_to_all x1, blocking collectives, on_device(): codes = lax.all_to_all(codes, 'x', split_axis=0, concat_axis=0, tiled=True)  27.7 us
    all_to_all x1, waiting for transfers between devices, on_device(): lax.all_to_all(amplitudes, ('x', 'z'), split_axis=1, concat_axis=0, tiled...  27.6 us
    all_to_all x1, blocking collectives, on_device(): lax.all_to_all(recode(codes), 'z', split_axis=0, concat_axis=0, tiled=True)  24.6 us
    pallas_call x1, Pallas kernels, ladder_codes(): pl.pallas_call(ladder_kernel, grid_spec=pltpu.PrefetchScalarGridSpec(num_...  12.9 us
    all_to_all x1, starting transfers between devices, on_device(): lax.all_to_all(amplitudes, ('x', 'z'), split_axis=1, concat_axis=0, tiled...  11.6 us
    pallas_call x1, Pallas kernels, arrange(): pl.pallas_call(arrange_kernel, grid_spec=pltpu.PrefetchScalarGridSpec(num...  10.6 us
    pallas_call x1, Pallas kernels, recode(): pl.pallas_call(recode_kernel, grid=(SECTORS,), in_specs=[pl.BlockSpec((A_...  5.67 us
  transfers between devices with their start and end apart: 5, of which 4 were waited for; matrix products, arithmetic and copies ran while one was open for 3% of the time, Pallas kernels for 6%

commit v1 on v0

--- a/solution.py
+++ b/solution.py
@@ -15,8 +15,9 @@
 PAD_SLOTS = 2 * PAIRS
 ROWS = 256
 CODE_ROWS = ROWS + 16
-STEP_PAIRS = 4
+STEP_PAIRS = 9
 STEPS = PAIRS // STEP_PAIRS
+AHEAD = 2
 TOP = 32760.0
 TINY = 1e-30
 GRAIN = 64.0
@@ -108,61 +109,82 @@
     return codes[:ROWS, :].astype(jnp.int32).astype(jnp.float32) * scale
 
 
-def ladder_kernel(order, pair_sector, *refs):
-    tiles, (w, out, acc) = refs[: 2 * STEP_PAIRS], refs[2 * STEP_PAIRS :]
-    step = pl.program_id(0)
-
-    @pl.when(step == 0)
-    def _():
-        acc[...] = jnp.zeros_like(acc)
-
-    for i in range(STEP_PAIRS):
-        s = pair_sector[step * STEP_PAIRS + i]
-        left = jnp.concatenate([tiles[2 * i][...], tiles[2 * i + 1][...]], axis=1)
-        right = w[2 * i : 2 * i + 2].reshape(2 * TILE, A_PER * TILE)
-        acc[s] += jnp.dot(left, right, preferred_element_type=jnp.float32)
-
-    @pl.when(step == STEPS - 1)
-    def _():
-        def encode(s, _):
-            for r in range(A_PER):
-                put_codes(out.at[r, s], acc[s, :, r * TILE : (r + 1) * TILE])
-            return 0
-
-        lax.fori_loop(0, SECTORS, encode, 0)
+def ladder_kernel(order, pair_sector, x_hbm, w_hbm, out, x, w, acc, x_sem, w_sem):
+    x_copy = pltpu.make_async_copy(x_hbm, x, x_sem)
+    x_copy.start()
+
+    def w_copy(k):
+        part = pl.ds(k * 2 * STEP_PAIRS, 2 * STEP_PAIRS)
+        return pltpu.make_async_copy(w_hbm.at[part], w.at[part], w_sem.at[k])
+
+    for k in range(AHEAD):
+        w_copy(k).start()
+    acc[...] = jnp.zeros_like(acc)
+    x_copy.wait()
+
+    def step(k, _):
+        @pl.when(k + AHEAD < STEPS)
+        def _():
+            w_copy(k + AHEAD).start()
+
+        w_copy(k).wait()
+        for i in range(STEP_PAIRS):
+            pair = k * STEP_PAIRS + i
+            s = pair_sector[pair]
+            first = pl.multiple_of(order[2 * pair] * TILE, TILE)
+            second = pl.multiple_of(order[2 * pair + 1] * TILE, TILE)
+            left = jnp.concatenate([x[:, pl.ds(first, TILE)], x[:, pl.ds(second, TILE)]], axis=1)
+            right = w[pl.ds(2 * pair, 2)].reshape(2 * TILE, A_PER * TILE)
+            acc[s] += jnp.dot(left, right, preferred_element_type=jnp.float32)
+        return 0
+
+    lax.fori_loop(0, STEPS, step, 0)
+
+    def encode(s, _):
+        for r in range(A_PER):
+            put_codes(out.at[r, s], acc[s, :, r * TILE : (r + 1) * TILE])
+        return 0
+
+    lax.fori_loop(0, SECTORS, encode, 0)
 
 
 def ladder_codes(order, pair_sector, x, w):
-    def tile(i):
-        return pl.BlockSpec((ROWS, TILE), lambda j, o, p: (0, o[j * 2 * STEP_PAIRS + i]))
-
     return pl.pallas_call(
         ladder_kernel,
-        grid_spec=pltpu.PrefetchScalarGridSpec(
-            num_scalar_prefetch=2,
-            grid=(STEPS,),
-            in_specs=[tile(i) for i in range(2 * STEP_PAIRS)]
-            + [pl.BlockSpec((2 * STEP_PAIRS, TILE, A_PER * TILE), lambda j, o, p: (j, 0, 0))],
-            out_specs=pl.BlockSpec((A_PER, SECTORS, CODE_ROWS, TILE), lambda j, o, p: (0, 0, 0, 0)),
-            scratch_shapes=[pltpu.VMEM((SECTORS, ROWS, A_PER * TILE), jnp.float32)],
-        ),
+        in_specs=[
+            pl.BlockSpec(memory_space=pltpu.SMEM),
+            pl.BlockSpec(memory_space=pltpu.SMEM),
+            pl.BlockSpec(memory_space=pl.ANY),
+            pl.BlockSpec(memory_space=pl.ANY),
+        ],
+        out_specs=pl.BlockSpec(memory_space=pltpu.VMEM),
+        scratch_shapes=[
+            pltpu.VMEM((ROWS, SLOTS * TILE), jnp.bfloat16),
+            pltpu.VMEM((PAD_SLOTS, TILE, A_PER * TILE), jnp.bfloat16),
+            pltpu.VMEM((SECTORS, ROWS, A_PER * TILE), jnp.float32),
+            pltpu.SemaphoreType.DMA,
+            pltpu.SemaphoreType.DMA((STEPS,)),
+        ],
         out_shape=jax.ShapeDtypeStruct((A_PER, SECTORS, CODE_ROWS, TILE), jnp.int16),
+        compiler_params=pltpu.CompilerParams(vmem_limit_bytes=58 * 2**20),
         cost_estimate=pl.CostEstimate(flops=2 * 36 * 256 * 256 * 512, bytes_accessed=16 * 2**20, transcendentals=0),
         name="ladder_codes",
-    )(order, pair_sector, *[x] * (2 * STEP_PAIRS), w)
+    )(order, pair_sector, x, w)
 
 
 def recode_kernel(codes, out):
-    put_codes(out.at[0], sum(get_codes(codes.at[i, 0]) for i in range(A_PER)))
+    def one(s, _):
+        put_codes(out.at[s], sum(get_codes(codes.at[i, s]) for i in range(A_PER)))
+        return 0
+
+    lax.fori_loop(0, SECTORS, one, 0)
 
 
 def recode(codes):
     return pl.pallas_call(
         recode_kernel,
-        grid=(SECTORS,),
-        in_specs=[pl.BlockSpec((A_PER, 1, CODE_ROWS, TILE), lambda j: (0, j, 0, 0))],
-        out_specs=pl.BlockSpec((1, CODE_ROWS, TILE), lambda j: (j, 0, 0)),
         out_shape=jax.ShapeDtypeStruct((SECTORS, CODE_ROWS, TILE), jnp.int16),
+        compiler_params=pltpu.CompilerParams(vmem_limit_bytes=16 * 2**20),
         name="recode",
     )(codes)
 
@@ -172,7 +194,7 @@
 
 
 def total(codes):
-    return pl.pallas_call(total_kernel, out_shape=jax.ShapeDtypeStruct((ROWS, TILE), jnp.bfloat16), name="total")(codes)
+    return pl.pallas_call(total_kernel, out_shape=jax.ShapeDtypeStruct((ROWS, TILE), jnp.bfloat16), name="total", compiler_params=pltpu.CompilerParams(vmem_limit_bytes=16 * 2**20))(codes)
 
 
 def on_device(amplitudes, integrals, out_tile, cd_slot):

time: 182 us -> 171 us (0.940)
  Pallas kernels: 31 us -> 20.2 us
    pallas_call x2, Pallas kernels: 18.6 us -> 10.2 us  [the longest x1 9.3 us: ladder_codes(): pl.pallas_call(ladder_kernel, in_specs=[pl.BlockSpec(memory_space=pltpu.S...]
  transfers between devices with their start and end apart: 5 -> 5, of which waited for: 4 -> 4; matrix products, arithmetic and copies ran while one was open for 3% -> 3% of each run, Pallas kernels for 6% -> 5%
where the time goes in v1:
time: 171 us; the launch traced here: 170 us
  waiting for transfers between devices  78.9 us (46%)
  blocking collectives  50.8 us (30%)
  Pallas kernels  20.2 us (12%)
  starting transfers between devices  14.6 us (9%)
  other arithmetic  4.51 us (3%)
    ppermute x3, waiting for transfers between devices, on_device(): lax.ppermute(mine, 'y', [(i, (i + d) % 4) for i in range(4)])  46 us
    all_to_all x1, waiting for transfers between devices, on_device(): lax.all_to_all(amplitudes, ('x', 'z'), split_axis=1, concat_axis=0, tiled...  29 us
    all_to_all x1, blocking collectives, on_device(): codes = lax.all_to_all(codes, 'x', split_axis=0, concat_axis=0, tiled=True)  26.9 us
    all_to_all x1, blocking collectives, on_device(): lax.all_to_all(recode(codes), 'z', split_axis=0, concat_axis=0, tiled=True)  23.9 us
    all_to_all x1, starting transfers between devices, on_device(): lax.all_to_all(amplitudes, ('x', 'z'), split_axis=1, concat_axis=0, tiled...  11.6 us
    pallas_call x1, Pallas kernels, ladder_codes(): pl.pallas_call(ladder_kernel, in_specs=[pl.BlockSpec(memory_space=pltpu.S...  9.3 us
    pallas_call x1, Pallas kernels, arrange(): pl.pallas_call(arrange_kernel, grid_spec=pltpu.PrefetchScalarGridSpec(num...  9.17 us
    ppermute x1, waiting for transfers between devices, on_device(): other_core = lax.ppermute(same_core, 'c', [(0, 1), (1, 0)])  3.97 us
  transfers between devices with their start and end apart: 5, of which 4 were waited for; matrix products, arithmetic and copies ran while one was open for 3% of the time, Pallas kernels for 5%

profile of v1, /device:TPU:16, one launch (start us, length us, event | category | flops | bytes accessed | tf_op | source)
XLA Modules:
  0.0 170.4 jit_solution(6611311800605994840)
XLA Ops:
  0.0 0.0 copy-start
  0.0 11.6 %all-to-all-start = ((bf16[8,32,8192]{2,0,1:T(8,128)(2,1)}), bf16[8,32,8192]{2,0,1:T(8,128)(2,1)}, u32[]{:S(2)}, u32[]{:S(2)}) async-start(bf16[8,32,8192]{2,0,1:T(8,128)(2,1)} %bitcast.7), calls=%async_computation | async-start | bytes 8388608 | tf_op jit(solution)/shard_map/all_to_all | solution.py:208
  11.6 0.0 copy-done
  11.6 0.0 copy-start.1
  11.6 0.0 copy-start.2
  11.6 1.4 collective-permute-start
  13.0 0.6 collective-permute-start.1
  13.6 1.1 collective-permute-start.2
  14.7 44.1 %collective-permute-done = bf16[32,128,128]{2,1,0:T(8,128)(2,1)S(1)} collective-permute-done((bf16[32,128,128]{2,1,0:T(8,128)(2,1)S(1)}, bf16[32,128,128]{2,1,0:T(8,128)(2,1)S(1)}, u32[]{:S(2)}, u32[]{:S(2)}) %collective-permute-start) | collective-permute-done | bytes 1048608 | tf_op jit(solution)/shard_map/ppermute | solution.py:204
  58.8 0.0 collective-permute-done.1
  58.8 1.8 %collective-permute-done.2 = bf16[32,128,128]{2,1,0:T(8,128)(2,1)S(1)} collective-permute-done((bf16[32,128,128]{2,1,0:T(8,128)(2,1)S(1)}, bf16[32,128,128]{2,1,0:T(8,128)(2,1)S(1)}, u32[]{:S(2)}, u32[]{:S(2)}) %collective-permute-start.2) | collective-permute-done | bytes 1048608 | tf_op jit(solution)/shard_map/ppermute | solution.py:204
  60.6 2.2 %pad_maximum_fusion.same_core = bf16[128,128,128]{2,1,0:T(8,128)(2,1)} fusion(bf16[32,128,128]{2,1,0:T(8,128)(2,1)S(1)} %collective-permute-done.2, bf16[32,128,128]{2,1,0:T(8,128)(2,1)S(1)} %collective-permute-done.1, bf16[32,128,128]{2,1,0:T(8,128)(2,1)S(1)} %collective-permute-done, bf16[32,128,128]{2,1,0:T(8,128)(2,1)S(1)} %bitcast.11), kind=kLoop, calls=%fused_computation | loop fusion | flops 6291456 | bytes 8388608 | tf_op jit(solution)/shard_map/concatenate | solution.py:205
  62.9 0.0 collective-permute-start.3
  62.9 0.0 copy-done.1
  62.9 0.0 copy-done.2
  62.9 0.2 select_reduce_fusion
  63.1 0.1 reshape.151
  63.2 0.1 reduce_sum.101
  63.3 0.1 fusion.5
  63.4 0.1 copy.5
  63.5 0.1 slice_reduce_fusion
  63.6 0.1 convert_reduce_fusion.3
  63.7 0.1 select_reduce_fusion.5
  63.8 0.2 convert_reduce_fusion.1
  64.0 0.1 select_reduce_fusion.4
  64.1 0.1 iota_compare_fusion.1
  64.2 0.1 select_reduce_fusion.2
  64.3 0.1 copy.6
  64.4 0.7 reshape.152.place
  65.1 0.7 convert_reduce_fusion
  65.8 0.1 convert_reduce_fusion.2
  65.9 0.5 broadcast_add_fusion.pair_sector
  66.4 4.0 %collective-permute-done.3.other_core = bf16[128,128,128]{2,1,0:T(8,128)(2,1)} collective-permute-done((bf16[128,128,128]{2,1,0:T(8,128)(2,1)}, bf16[128,128,128]{2,1,0:T(8,128)(2,1)}, u32[]{:S(2)}, u32[]{:S(2)}) %collective-permute-start.3) | collective-permute-done | bytes 4194336 | tf_op jit(solution)/shard_map/ppermute | solution.py:206
  70.4 9.2 %arrange.1.w_hbm = bf16[72,128,512]{2,1,0:T(8,128)(2,1)} custom-call(s32[72]{0:T(128)} %get-tuple-element.7.valid, s32[288]{0:T(512)} %reshape.152.place, bf16[128,128,128]{2,1,0:T(8,128)(2,1)} %pad_maximum_fusion.same_core, bf16[128,128,128]{2,1,0:T(8,128)(2,1)} %collective-permute-done.3.other_core), custom_call_target="tpu_custom_call" | custom-call | bytes 18874368 | tf_op jit(solution)/shard_map/arrange/pallas_call | solution.py:80
  79.6 29.0 %all-to-all-done = bf16[8,32,8192]{2,0,1:T(8,128)(2,1)} async-done(((bf16[8,32,8192]{2,0,1:T(8,128)(2,1)}), bf16[8,32,8192]{2,0,1:T(8,128)(2,1)}, u32[]{:S(2)}, u32[]{:S(2)}) %all-to-all-start) | async-done | bytes 4194336 | tf_op jit(solution)/shard_map/all_to_all | solution.py:208
  108.6 9.3 %ladder_codes.1 = s16[4,8,272,128]{3,2,1,0:T(8,128)(2,1)} custom-call(s32[72]{0:T(128)} %get-tuple-element.8.order, s32[36]{0:T(128)} %broadcast_add_fusion.pair_sector, bf16[256,8192]{1,0:T(8,128)(2,1)} %bitcast.4.x_hbm, bf16[72,128,512]{2,1,0:T(8,128)(2,1)} %arrange.1.w_hbm), custom_call_target="tpu_custom_call" | custom-call | flops 2415919104 | bytes 16777216 | tf_op jit(solution)/shard_map/ladder_codes/pallas_call | solution.py:152
  117.9 26.9 %all_to_all.29.codes = s16[4,8,272,128]{3,2,1,0:T(8,128)(2,1)S(1)} all-to-all(s16[4,8,272,128]{3,2,1,0:T(8,128)(2,1)} %ladder_codes.1), channel_id=1, replica_groups=mesh['y'=4,'c'=2,'x'=4,'z'=8] {'x'}, dimensions={0} | all-to-all | bytes 4456448 | tf_op jit(solution)/shard_map/all_to_all | solution.py:210
  144.8 0.9 recode.1
  145.7 23.9 %all_to_all.30.codes = s16[8,272,128]{2,1,0:T(8,128)(2,1)S(1)} all-to-all(s16[8,272,128]{2,1,0:T(8,128)(2,1)S(1)} %recode.1), channel_id=1, replica_groups=mesh['y'=4,'c'=2,'x'=4,'z'=8] {'z'}, dimensions={0} | all-to-all | bytes 1114112 | tf_op jit(solution)/shard_map/all_to_all | solution.py:211
  169.6 0.8 total.1
  (4 shorter events, 0.0 us)
Async XLA Ops:
  0.0 11.6 %copy-start = (bf16[1,32,128,128]{3,2,1,0:T(8,128)(2,1)S(1)}, bf16[1,32,128,128]{3,2,1,0:T(8,128)(2,1)}, u32[]{:S(2)}) copy-start(bf16[1,32,128,128]{3,2,1,0:T(8,128)(2,1)} %param.5) | copy-start | bytes 3145732
  0.0 108.6 %all-to-all-start = ((bf16[8,32,8192]{2,0,1:T(8,128)(2,1)}), bf16[8,32,8192]{2,0,1:T(8,128)(2,1)}, u32[]{:S(2)}, u32[]{:S(2)}) async-start(bf16[8,32,8192]{2,0,1:T(8,128)(2,1)} %bitcast.7), calls=%async_computation | async-start | bytes 8388608 | tf_op jit(solution)/shard_map/all_to_all | solution.py:208
  11.6 51.3 %copy-start.1 = (s32[1,256]{1,0:T(1,128)S(1)}, s32[1,256]{1,0:T(1,128)}, u32[]{:S(2)}) copy-start(s32[1,256]{1,0:T(1,128)} %param.6) | copy-start | bytes 3076
  11.6 51.3 %copy-start.2 = (s32[1,256]{1,0:T(1,128)S(1)}, s32[1,256]{1,0:T(1,128)}, u32[]{:S(2)}) copy-start(s32[1,256]{1,0:T(1,128)} %param.7) | copy-start | bytes 3076
  11.6 47.2 %collective-permute-start = (bf16[32,128,128]{2,1,0:T(8,128)(2,1)S(1)}, bf16[32,128,128]{2,1,0:T(8,128)(2,1)S(1)}, u32[]{:S(2)}, u32[]{:S(2)}) collective-permute-start(bf16[32,128,128]{2,1,0:T(8,128)(2,1)S(1)} %bitcast.8), channel_id=1, source_target_pairs={{0,64},{64,128},{128,192},{192,0},{1,65},{65,129},{129,193},{193,1... | collective-permute-start | bytes 3145736 | tf_op jit(solution)/shard_map/ppermute | solution.py:204
  13.0 45.8 %collective-permute-start.1 = (bf16[32,128,128]{2,1,0:T(8,128)(2,1)S(1)}, bf16[32,128,128]{2,1,0:T(8,128)(2,1)S(1)}, u32[]{:S(2)}, u32[]{:S(2)}) collective-permute-start(bf16[32,128,128]{2,1,0:T(8,128)(2,1)S(1)} %bitcast.9), channel_id=1, source_target_pairs={{0,128},{64,192},{128,0},{192,64},{1,129},{65,193},{129,1},{193,65... | collective-permute-start | bytes 3145736 | tf_op jit(solution)/shard_map/ppermute | solution.py:204
  13.6 47.0 %collective-permute-start.2 = (bf16[32,128,128]{2,1,0:T(8,128)(2,1)S(1)}, bf16[32,128,128]{2,1,0:T(8,128)(2,1)S(1)}, u32[]{:S(2)}, u32[]{:S(2)}) collective-permute-start(bf16[32,128,128]{2,1,0:T(8,128)(2,1)S(1)} %bitcast.10), channel_id=1, source_target_pairs={{0,192},{64,0},{128,64},{192,128},{1,193},{65,1},{129,65},{193,129... | collective-permute-start | bytes 3145736 | tf_op jit(solution)/shard_map/ppermute | solution.py:204
  62.9 7.5 %collective-permute-start.3 = (bf16[128,128,128]{2,1,0:T(8,128)(2,1)}, bf16[128,128,128]{2,1,0:T(8,128)(2,1)}, u32[]{:S(2)}, u32[]{:S(2)}) collective-permute-start(bf16[128,128,128]{2,1,0:T(8,128)(2,1)} %pad_maximum_fusion.same_core), channel_id=1, source_target_pairs={{0,32},{32,0},{1,33},{33,1},{2,34},{34,2},{3,35},{35,3},{4,36},{36... | collective-permute-start | bytes 12582920 | tf_op jit(solution)/shard_map/ppermute | solution.py:206

commit v2 on v1

--- a/solution.py
+++ b/solution.py
@@ -14,10 +14,12 @@
 PAIRS = (SLOTS + SECTORS) // 2
 PAD_SLOTS = 2 * PAIRS
 ROWS = 256
-CODE_ROWS = ROWS + 16
+CODE_ROWS = ROWS + 8
 STEP_PAIRS = 9
 STEPS = PAIRS // STEP_PAIRS
 AHEAD = 2
+NEAR = 8
+FAR = 4
 TOP = 32760.0
 TINY = 1e-30
 GRAIN = 64.0
@@ -142,7 +144,7 @@
 
     def encode(s, _):
         for r in range(A_PER):
-            put_codes(out.at[r, s], acc[s, :, r * TILE : (r + 1) * TILE])
+            put_codes(out.at[r * 2 + s % 2, s // 2], acc[s, :, r * TILE : (r + 1) * TILE])
         return 0
 
     lax.fori_loop(0, SECTORS, encode, 0)
@@ -165,7 +167,7 @@
             pltpu.SemaphoreType.DMA,
             pltpu.SemaphoreType.DMA((STEPS,)),
         ],
-        out_shape=jax.ShapeDtypeStruct((A_PER, SECTORS, CODE_ROWS, TILE), jnp.int16),
+        out_shape=jax.ShapeDtypeStruct((NEAR, FAR, CODE_ROWS, TILE), jnp.int16),
         compiler_params=pltpu.CompilerParams(vmem_limit_bytes=58 * 2**20),
         cost_estimate=pl.CostEstimate(flops=2 * 36 * 256 * 256 * 512, bytes_accessed=16 * 2**20, transcendentals=0),
         name="ladder_codes",
@@ -174,23 +176,23 @@
 
 def recode_kernel(codes, out):
     def one(s, _):
-        put_codes(out.at[s], sum(get_codes(codes.at[i, s]) for i in range(A_PER)))
+        put_codes(out.at[s], sum(get_codes(codes.at[i, s]) for i in range(NEAR)))
         return 0
 
-    lax.fori_loop(0, SECTORS, one, 0)
+    lax.fori_loop(0, FAR, one, 0)
 
 
 def recode(codes):
     return pl.pallas_call(
         recode_kernel,
-        out_shape=jax.ShapeDtypeStruct((SECTORS, CODE_ROWS, TILE), jnp.int16),
+        out_shape=jax.ShapeDtypeStruct((FAR, CODE_ROWS, TILE), jnp.int16),
         compiler_params=pltpu.CompilerParams(vmem_limit_bytes=16 * 2**20),
         name="recode",
     )(codes)
 
 
 def total_kernel(codes, out):
-    out[...] = sum(get_codes(codes.at[i]) for i in range(SECTORS)).astype(jnp.bfloat16)
+    out[...] = sum(get_codes(codes.at[i]) for i in range(FAR)).astype(jnp.bfloat16)
 
 
 def total(codes):
@@ -205,15 +207,15 @@
     same_core = jnp.concatenate(same_core, axis=0)
     other_core = lax.ppermute(same_core, "c", [(0, 1), (1, 0)])
     w = arrange(valid, place, same_core, other_core)
-    exchanged = lax.all_to_all(amplitudes, ("x", "z"), split_axis=1, concat_axis=0, tiled=True)
+    exchanged = lax.all_to_all(amplitudes, ("x", "h", "l"), split_axis=1, concat_axis=0, tiled=True)
     codes = ladder_codes(order, pair_sector, exchanged, w)
-    codes = lax.all_to_all(codes, "x", split_axis=0, concat_axis=0, tiled=True)
-    codes = lax.all_to_all(recode(codes), "z", split_axis=0, concat_axis=0, tiled=True)
+    codes = lax.all_to_all(codes, ("x", "l"), split_axis=0, concat_axis=0, tiled=True)
+    codes = lax.all_to_all(recode(codes), "h", split_axis=0, concat_axis=0, tiled=True)
     return total(codes)
 
 
 def solution(mesh):
-    grid = Mesh(mesh.devices.reshape(4, 2, 4, 8), ("y", "c", "x", "z"))
-    blk, wide = ("y", "c"), ("x", "z")
+    grid = Mesh(mesh.devices.reshape(4, 2, 4, 4, 2), ("y", "c", "x", "h", "l"))
+    blk, wide = ("y", "c"), ("x", "h", "l")
     in_specs = (P(blk + wide, None), P(wide, blk, None, None), P(wide, None), P(wide, None))
     return jax.shard_map(on_device, mesh=grid, in_specs=in_specs, out_specs=P(blk, wide), check_vma=False)

time: 171 us -> 164 us (0.959)
  blocking collectives: 50.8 us -> 44.7 us
    all_to_all x2, blocking collectives: 50.8 us -> 44.7 us  [the longest x1 31 us: on_device(): lax.all_to_all(codes, ('x', 'l'), split_axis=0, concat_axis=0, tiled=True)]
  transfers between devices with their start and end apart: 5 -> 5, of which waited for: 4 -> 4; matrix products, arithmetic and copies ran while one was open for 3% -> 3% of each run, Pallas kernels for 5% -> 6%
where the time goes in v2:
time: 164 us
  waiting for transfers between devices  79 us (48%)
  blocking collectives  44.7 us (27%)
  Pallas kernels  20 us (12%)
  starting transfers between devices  14.6 us (9%)
  other arithmetic  4.51 us (3%)
    ppermute x3, waiting for transfers between devices, on_device(): lax.ppermute(mine, 'y', [(i, (i + d) % 4) for i in range(4)])  46 us
    all_to_all x1, blocking collectives, on_device(): lax.all_to_all(codes, ('x', 'l'), split_axis=0, concat_axis=0, tiled=True)  31 us
    all_to_all x1, waiting for transfers between devices, on_device(): lax.all_to_all(amplitudes, ('x', 'h', 'l'), split_axis=1, concat_axis=0,...  29 us
    all_to_all x1, blocking collectives, on_device(): lax.all_to_all(recode(codes), 'h', split_axis=0, concat_axis=0, tiled=True)  13.7 us
    all_to_all x1, starting transfers between devices, on_device(): lax.all_to_all(amplitudes, ('x', 'h', 'l'), split_axis=1, concat_axis=0,...  11.6 us
    pallas_call x1, Pallas kernels, ladder_codes(): pl.pallas_call(ladder_kernel, in_specs=[pl.BlockSpec(memory_space=pltpu.S...  9.32 us
    pallas_call x1, Pallas kernels, arrange(): pl.pallas_call(arrange_kernel, grid_spec=pltpu.PrefetchScalarGridSpec(num...  9.16 us
    ppermute x1, waiting for transfers between devices, on_device(): other_core = lax.ppermute(same_core, 'c', [(0, 1), (1, 0)])  3.97 us
  transfers between devices with their start and end apart: 5, of which 4 were waited for; matrix products, arithmetic and copies ran while one was open for 3% of the time, Pallas kernels for 6%

profile of v2, /device:TPU:16, one launch (start us, length us, event | category | flops | bytes accessed | tf_op | source)
XLA Modules:
  0.0 164.1 jit_solution(13317712676609815319)
XLA Ops:
  0.0 0.0 copy-start
  0.0 11.6 %all-to-all-start = ((bf16[8,32,8192]{2,0,1:T(8,128)(2,1)}), bf16[8,32,8192]{2,0,1:T(8,128)(2,1)}, u32[]{:S(2)}, u32[]{:S(2)}) async-start(bf16[8,32,8192]{2,0,1:T(8,128)(2,1)} %bitcast.7), calls=%async_computation | async-start | bytes 8388608 | tf_op jit(solution)/shard_map/all_to_all | solution.py:210
  11.6 0.0 copy-done
  11.6 0.0 copy-start.1
  11.6 0.0 copy-start.2
  11.6 1.4 collective-permute-start
  13.0 0.6 collective-permute-start.1
  13.6 1.1 collective-permute-start.2
  14.7 44.1 %collective-permute-done = bf16[32,128,128]{2,1,0:T(8,128)(2,1)S(1)} collective-permute-done((bf16[32,128,128]{2,1,0:T(8,128)(2,1)S(1)}, bf16[32,128,128]{2,1,0:T(8,128)(2,1)S(1)}, u32[]{:S(2)}, u32[]{:S(2)}) %collective-permute-start) | collective-permute-done | bytes 1048608 | tf_op jit(solution)/shard_map/ppermute | solution.py:206
  58.8 0.0 collective-permute-done.1
  58.8 1.8 %collective-permute-done.2 = bf16[32,128,128]{2,1,0:T(8,128)(2,1)S(1)} collective-permute-done((bf16[32,128,128]{2,1,0:T(8,128)(2,1)S(1)}, bf16[32,128,128]{2,1,0:T(8,128)(2,1)S(1)}, u32[]{:S(2)}, u32[]{:S(2)}) %collective-permute-start.2) | collective-permute-done | bytes 1048608 | tf_op jit(solution)/shard_map/ppermute | solution.py:206
  60.6 2.2 %pad_maximum_fusion.same_core = bf16[128,128,128]{2,1,0:T(8,128)(2,1)} fusion(bf16[32,128,128]{2,1,0:T(8,128)(2,1)S(1)} %collective-permute-done.2, bf16[32,128,128]{2,1,0:T(8,128)(2,1)S(1)} %collective-permute-done.1, bf16[32,128,128]{2,1,0:T(8,128)(2,1)S(1)} %collective-permute-done, bf16[32,128,128]{2,1,0:T(8,128)(2,1)S(1)} %bitcast.11), kind=kLoop, calls=%fused_computation | loop fusion | flops 6291456 | bytes 8388608 | tf_op jit(solution)/shard_map/concatenate | solution.py:207
  62.9 0.0 collective-permute-start.3
  62.9 0.0 copy-done.1
  62.9 0.0 copy-done.2
  62.9 0.2 select_reduce_fusion
  63.1 0.1 reshape.151
  63.2 0.1 reduce_sum.101
  63.3 0.1 fusion.5
  63.4 0.1 copy.5
  63.5 0.1 slice_reduce_fusion
  63.6 0.1 convert_reduce_fusion.3
  63.7 0.1 select_reduce_fusion.5
  63.8 0.2 convert_reduce_fusion.1
  64.0 0.1 select_reduce_fusion.4
  64.1 0.1 iota_compare_fusion.1
  64.2 0.1 select_reduce_fusion.2
  64.3 0.1 copy.6
  64.4 0.7 reshape.152.place
  65.1 0.7 convert_reduce_fusion
  65.8 0.1 convert_reduce_fusion.2
  65.9 0.5 broadcast_add_fusion.pair_sector
  66.4 4.0 %collective-permute-done.3.other_core = bf16[128,128,128]{2,1,0:T(8,128)(2,1)} collective-permute-done((bf16[128,128,128]{2,1,0:T(8,128)(2,1)}, bf16[128,128,128]{2,1,0:T(8,128)(2,1)}, u32[]{:S(2)}, u32[]{:S(2)}) %collective-permute-start.3) | collective-permute-done | bytes 4194336 | tf_op jit(solution)/shard_map/ppermute | solution.py:208
  70.4 9.2 %arrange.1.w_hbm = bf16[72,128,512]{2,1,0:T(8,128)(2,1)} custom-call(s32[72]{0:T(128)} %get-tuple-element.7.valid, s32[288]{0:T(512)} %reshape.152.place, bf16[128,128,128]{2,1,0:T(8,128)(2,1)} %pad_maximum_fusion.same_core, bf16[128,128,128]{2,1,0:T(8,128)(2,1)} %collective-permute-done.3.other_core), custom_call_target="tpu_custom_call" | custom-call | bytes 18874368 | tf_op jit(solution)/shard_map/arrange/pallas_call | solution.py:82
  79.5 29.0 %all-to-all-done = bf16[8,32,8192]{2,0,1:T(8,128)(2,1)} async-done(((bf16[8,32,8192]{2,0,1:T(8,128)(2,1)}), bf16[8,32,8192]{2,0,1:T(8,128)(2,1)}, u32[]{:S(2)}, u32[]{:S(2)}) %all-to-all-start) | async-done | bytes 4194336 | tf_op jit(solution)/shard_map/all_to_all | solution.py:210
  108.6 9.3 %ladder_codes.1 = s16[8,4,264,128]{3,2,1,0:T(8,128)(2,1)} custom-call(s32[72]{0:T(128)} %get-tuple-element.8.order, s32[36]{0:T(128)} %broadcast_add_fusion.pair_sector, bf16[256,8192]{1,0:T(8,128)(2,1)} %bitcast.4.x_hbm, bf16[72,128,512]{2,1,0:T(8,128)(2,1)} %arrange.1.w_hbm), custom_call_target="tpu_custom_call" | custom-call | flops 2415919104 | bytes 16777216 | tf_op jit(solution)/shard_map/ladder_codes/pallas_call | solution.py:154
  117.9 31.0 %all_to_all.29.codes = s16[8,4,264,128]{3,2,1,0:T(8,128)(2,1)S(1)} all-to-all(s16[8,4,264,128]{3,2,1,0:T(8,128)(2,1)} %ladder_codes.1), channel_id=1, replica_groups=mesh['y'=4,'c'=2,'x'=4,'h'=4,'l'=2] {'x','l'}, dimensions={0} | all-to-all | bytes 4325376 | tf_op jit(solution)/shard_map/all_to_all | solution.py:212
  148.9 0.8 recode.1
  149.7 13.7 %all_to_all.30.codes = s16[4,264,128]{2,1,0:T(8,128)(2,1)S(1)} all-to-all(s16[4,264,128]{2,1,0:T(8,128)(2,1)S(1)} %recode.1), channel_id=1, replica_groups=mesh['y'=4,'c'=2,'x'=4,'h'=4,'l'=2] {'h'}, dimensions={0} | all-to-all | bytes 540672 | tf_op jit(solution)/shard_map/all_to_all | solution.py:213
  163.4 0.7 total.1
  (4 shorter events, 0.0 us)
Async XLA Ops:
  0.0 11.6 %copy-start = (bf16[1,32,128,128]{3,2,1,0:T(8,128)(2,1)S(1)}, bf16[1,32,128,128]{3,2,1,0:T(8,128)(2,1)}, u32[]{:S(2)}) copy-start(bf16[1,32,128,128]{3,2,1,0:T(8,128)(2,1)} %param.5) | copy-start | bytes 3145732
  0.0 108.6 %all-to-all-start = ((bf16[8,32,8192]{2,0,1:T(8,128)(2,1)}), bf16[8,32,8192]{2,0,1:T(8,128)(2,1)}, u32[]{:S(2)}, u32[]{:S(2)}) async-start(bf16[8,32,8192]{2,0,1:T(8,128)(2,1)} %bitcast.7), calls=%async_computation | async-start | bytes 8388608 | tf_op jit(solution)/shard_map/all_to_all | solution.py:210
  11.6 51.3 %copy-start.1 = (s32[1,256]{1,0:T(1,128)S(1)}, s32[1,256]{1,0:T(1,128)}, u32[]{:S(2)}) copy-start(s32[1,256]{1,0:T(1,128)} %param.6) | copy-start | bytes 3076
  11.6 51.3 %copy-start.2 = (s32[1,256]{1,0:T(1,128)S(1)}, s32[1,256]{1,0:T(1,128)}, u32[]{:S(2)}) copy-start(s32[1,256]{1,0:T(1,128)} %param.7) | copy-start | bytes 3076
  11.6 47.2 %collective-permute-start = (bf16[32,128,128]{2,1,0:T(8,128)(2,1)S(1)}, bf16[32,128,128]{2,1,0:T(8,128)(2,1)S(1)}, u32[]{:S(2)}, u32[]{:S(2)}) collective-permute-start(bf16[32,128,128]{2,1,0:T(8,128)(2,1)S(1)} %bitcast.8), channel_id=1, source_target_pairs={{0,64},{64,128},{128,192},{192,0},{1,65},{65,129},{129,193},{193,1... | collective-permute-start | bytes 3145736 | tf_op jit(solution)/shard_map/ppermute | solution.py:206
  13.0 45.8 %collective-permute-start.1 = (bf16[32,128,128]{2,1,0:T(8,128)(2,1)S(1)}, bf16[32,128,128]{2,1,0:T(8,128)(2,1)S(1)}, u32[]{:S(2)}, u32[]{:S(2)}) collective-permute-start(bf16[32,128,128]{2,1,0:T(8,128)(2,1)S(1)} %bitcast.9), channel_id=1, source_target_pairs={{0,128},{64,192},{128,0},{192,64},{1,129},{65,193},{129,1},{193,65... | collective-permute-start | bytes 3145736 | tf_op jit(solution)/shard_map/ppermute | solution.py:206
  13.6 47.0 %collective-permute-start.2 = (bf16[32,128,128]{2,1,0:T(8,128)(2,1)S(1)}, bf16[32,128,128]{2,1,0:T(8,128)(2,1)S(1)}, u32[]{:S(2)}, u32[]{:S(2)}) collective-permute-start(bf16[32,128,128]{2,1,0:T(8,128)(2,1)S(1)} %bitcast.10), channel_id=1, source_target_pairs={{0,192},{64,0},{128,64},{192,128},{1,193},{65,1},{129,65},{193,129... | collective-permute-start | bytes 3145736 | tf_op jit(solution)/shard_map/ppermute | solution.py:206
  62.9 7.5 %collective-permute-start.3 = (bf16[128,128,128]{2,1,0:T(8,128)(2,1)}, bf16[128,128,128]{2,1,0:T(8,128)(2,1)}, u32[]{:S(2)}, u32[]{:S(2)}) collective-permute-start(bf16[128,128,128]{2,1,0:T(8,128)(2,1)} %pad_maximum_fusion.same_core), channel_id=1, source_target_pairs={{0,32},{32,0},{1,33},{33,1},{2,34},{34,2},{3,35},{35,3},{4,36},{36... | collective-permute-start | bytes 12582920 | tf_op jit(solution)/shard_map/ppermute | solution.py:208

commit v3 on v2

--- a/solution.py
+++ b/solution.py
@@ -168,7 +168,7 @@
             pltpu.SemaphoreType.DMA((STEPS,)),
         ],
         out_shape=jax.ShapeDtypeStruct((NEAR, FAR, CODE_ROWS, TILE), jnp.int16),
-        compiler_params=pltpu.CompilerParams(vmem_limit_bytes=58 * 2**20),
+        compiler_params=pltpu.CompilerParams(vmem_limit_bytes=44 * 2**20),
         cost_estimate=pl.CostEstimate(flops=2 * 36 * 256 * 256 * 512, bytes_accessed=16 * 2**20, transcendentals=0),
         name="ladder_codes",
     )(order, pair_sector, x, w)

time: 164 us -> 163 us (level)
  no operation moved by 1% of the time
where the time goes in v3:
time: 163 us; the launch traced here: 162 us
  waiting for transfers between devices  79.5 us (49%)
  blocking collectives  44.5 us (27%)
  Pallas kernels  18.5 us (11%)
  starting transfers between devices  14.6 us (9%)
  other arithmetic  3.98 us (2%)
    ppermute x3, waiting for transfers between devices, on_device(): lax.ppermute(mine, 'y', [(i, (i + d) % 4) for i in range(4)])  46 us
    all_to_all x1, blocking collectives, on_device(): lax.all_to_all(codes, ('x', 'l'), split_axis=0, concat_axis=0, tiled=True)  31 us
    all_to_all x1, waiting for transfers between devices, on_device(): lax.all_to_all(amplitudes, ('x', 'h', 'l'), split_axis=1, concat_axis=0,...  29 us
    all_to_all x1, blocking collectives, on_device(): lax.all_to_all(recode(codes), 'h', split_axis=0, concat_axis=0, tiled=True)  13.5 us
    all_to_all x1, starting transfers between devices, on_device(): lax.all_to_all(amplitudes, ('x', 'h', 'l'), split_axis=1, concat_axis=0,...  11.6 us
    pallas_call x1, Pallas kernels, arrange(): pl.pallas_call(arrange_kernel, grid_spec=pltpu.PrefetchScalarGridSpec(num...  9.19 us
    pallas_call x1, Pallas kernels, ladder_codes(): pl.pallas_call(ladder_kernel, in_specs=[pl.BlockSpec(memory_space=pltpu.S...  7.85 us
    ppermute x1, waiting for transfers between devices, on_device(): other_core = lax.ppermute(same_core, 'c', [(0, 1), (1, 0)])  4.51 us
  transfers between devices with their start and end apart: 5, of which 4 were waited for; matrix products, arithmetic and copies ran while one was open for 3% of the time, Pallas kernels for 6%

profile of v3, /device:TPU:16, one launch (start us, length us, event | category | flops | bytes accessed | tf_op | source)
XLA Modules:
  0.0 162.4 jit_solution(7234169646343142261)
XLA Ops:
  0.0 0.0 copy-start
  0.0 11.6 %all-to-all-start = ((bf16[8,32,8192]{2,0,1:T(8,128)(2,1)}), bf16[8,32,8192]{2,0,1:T(8,128)(2,1)}, u32[]{:S(2)}, u32[]{:S(2)}) async-start(bf16[8,32,8192]{2,0,1:T(8,128)(2,1)} %bitcast.7), calls=%async_computation | async-start | bytes 8388608 | tf_op jit(solution)/shard_map/all_to_all | solution.py:210
  11.6 0.0 copy-done
  11.6 0.0 copy-start.1
  11.6 0.0 copy-start.2
  11.6 1.4 collective-permute-start
  13.0 0.6 collective-permute-start.1
  13.6 1.1 collective-permute-start.2
  14.7 44.1 %collective-permute-done = bf16[32,128,128]{2,1,0:T(8,128)(2,1)S(1)} collective-permute-done((bf16[32,128,128]{2,1,0:T(8,128)(2,1)S(1)}, bf16[32,128,128]{2,1,0:T(8,128)(2,1)S(1)}, u32[]{:S(2)}, u32[]{:S(2)}) %collective-permute-start) | collective-permute-done | bytes 1048608 | tf_op jit(solution)/shard_map/ppermute | solution.py:206
  58.8 0.0 collective-permute-done.1
  58.8 1.8 %collective-permute-done.2 = bf16[32,128,128]{2,1,0:T(8,128)(2,1)S(1)} collective-permute-done((bf16[32,128,128]{2,1,0:T(8,128)(2,1)S(1)}, bf16[32,128,128]{2,1,0:T(8,128)(2,1)S(1)}, u32[]{:S(2)}, u32[]{:S(2)}) %collective-permute-start.2) | collective-permute-done | bytes 1048608 | tf_op jit(solution)/shard_map/ppermute | solution.py:206
  60.6 2.2 %pad_maximum_fusion.same_core = bf16[128,128,128]{2,1,0:T(8,128)(2,1)} fusion(bf16[32,128,128]{2,1,0:T(8,128)(2,1)S(1)} %collective-permute-done.2, bf16[32,128,128]{2,1,0:T(8,128)(2,1)S(1)} %collective-permute-done.1, bf16[32,128,128]{2,1,0:T(8,128)(2,1)S(1)} %collective-permute-done, bf16[32,128,128]{2,1,0:T(8,128)(2,1)S(1)} %bitcast.11), kind=kLoop, calls=%fused_computation | loop fusion | flops 6291456 | bytes 8388608 | tf_op jit(solution)/shard_map/concatenate | solution.py:207
  62.9 0.0 collective-permute-start.3
  62.9 0.0 copy-done.1
  62.9 0.0 copy-done.2
  62.9 0.2 select_reduce_fusion
  63.1 0.1 reshape.151
  63.2 0.1 reduce_sum.101
  63.3 0.1 fusion.5
  63.4 0.1 copy.5
  63.5 0.1 slice_reduce_fusion
  63.6 0.1 convert_reduce_fusion.3
  63.7 0.1 select_reduce_fusion.5
  63.8 0.2 convert_reduce_fusion.1
  64.0 0.1 select_reduce_fusion.4
  64.1 0.1 iota_compare_fusion.1
  64.2 0.1 select_reduce_fusion.2
  64.3 0.1 copy.6
  64.4 0.7 reshape.152.place
  65.1 0.7 convert_reduce_fusion
  65.8 0.1 convert_reduce_fusion.2
  65.9 4.5 %collective-permute-done.3.other_core = bf16[128,128,128]{2,1,0:T(8,128)(2,1)} collective-permute-done((bf16[128,128,128]{2,1,0:T(8,128)(2,1)}, bf16[128,128,128]{2,1,0:T(8,128)(2,1)}, u32[]{:S(2)}, u32[]{:S(2)}) %collective-permute-start.3) | collective-permute-done | bytes 4194336 | tf_op jit(solution)/shard_map/ppermute | solution.py:208
  70.4 9.2 %arrange.1.w_hbm = bf16[72,128,512]{2,1,0:T(8,128)(2,1)} custom-call(s32[72]{0:T(128)} %get-tuple-element.7.valid, s32[288]{0:T(512)} %reshape.152.place, bf16[128,128,128]{2,1,0:T(8,128)(2,1)} %pad_maximum_fusion.same_core, bf16[128,128,128]{2,1,0:T(8,128)(2,1)} %collective-permute-done.3.other_core), custom_call_target="tpu_custom_call" | custom-call | bytes 18874368 | tf_op jit(solution)/shard_map/arrange/pallas_call | solution.py:82
  79.6 29.0 %all-to-all-done = bf16[8,32,8192]{2,0,1:T(8,128)(2,1)} async-done(((bf16[8,32,8192]{2,0,1:T(8,128)(2,1)}), bf16[8,32,8192]{2,0,1:T(8,128)(2,1)}, u32[]{:S(2)}, u32[]{:S(2)}) %all-to-all-start) | async-done | bytes 4194336 | tf_op jit(solution)/shard_map/all_to_all | solution.py:210
  108.6 7.9 %ladder_codes.1 = s16[8,4,264,128]{3,2,1,0:T(8,128)(2,1)S(1)} custom-call(s32[72]{0:T(128)S(1)} %get-tuple-element.8.order, s32[36]{0:T(128)S(1)} %broadcast_add_fusion.pair_sector, bf16[256,8192]{1,0:T(8,128)(2,1)} %bitcast.4.x_hbm, bf16[72,128,512]{2,1,0:T(8,128)(2,1)} %arrange.1.w_hbm), custom_call_target="tpu_custom_call" | custom-call | flops 2415919104 | bytes 16777216 | tf_op jit(solution)/shard_map/ladder_codes/pallas_call | solution.py:154
  116.4 31.0 %all_to_all.29.codes = s16[8,4,264,128]{3,2,1,0:T(8,128)(2,1)S(1)} all-to-all(s16[8,4,264,128]{3,2,1,0:T(8,128)(2,1)S(1)} %ladder_codes.1), channel_id=1, replica_groups=mesh['y'=4,'c'=2,'x'=4,'h'=4,'l'=2] {'x','l'}, dimensions={0} | all-to-all | bytes 4325376 | tf_op jit(solution)/shard_map/all_to_all | solution.py:212
  147.4 0.8 recode.1
  148.2 13.5 %all_to_all.30.codes = s16[4,264,128]{2,1,0:T(8,128)(2,1)S(1)} all-to-all(s16[4,264,128]{2,1,0:T(8,128)(2,1)S(1)} %recode.1), channel_id=1, replica_groups=mesh['y'=4,'c'=2,'x'=4,'h'=4,'l'=2] {'h'}, dimensions={0} | all-to-all | bytes 540672 | tf_op jit(solution)/shard_map/all_to_all | solution.py:213
  161.7 0.7 total.1
  (5 shorter events, 0.0 us)
Async XLA Ops:
  0.0 11.6 %copy-start = (bf16[1,32,128,128]{3,2,1,0:T(8,128)(2,1)S(1)}, bf16[1,32,128,128]{3,2,1,0:T(8,128)(2,1)}, u32[]{:S(2)}) copy-start(bf16[1,32,128,128]{3,2,1,0:T(8,128)(2,1)} %param.5) | copy-start | bytes 3145732
  0.0 108.6 %all-to-all-start = ((bf16[8,32,8192]{2,0,1:T(8,128)(2,1)}), bf16[8,32,8192]{2,0,1:T(8,128)(2,1)}, u32[]{:S(2)}, u32[]{:S(2)}) async-start(bf16[8,32,8192]{2,0,1:T(8,128)(2,1)} %bitcast.7), calls=%async_computation | async-start | bytes 8388608 | tf_op jit(solution)/shard_map/all_to_all | solution.py:210
  11.6 51.3 %copy-start.1 = (s32[1,256]{1,0:T(1,128)S(1)}, s32[1,256]{1,0:T(1,128)}, u32[]{:S(2)}) copy-start(s32[1,256]{1,0:T(1,128)} %param.6) | copy-start | bytes 3076
  11.6 51.3 %copy-start.2 = (s32[1,256]{1,0:T(1,128)S(1)}, s32[1,256]{1,0:T(1,128)}, u32[]{:S(2)}) copy-start(s32[1,256]{1,0:T(1,128)} %param.7) | copy-start | bytes 3076
  11.6 47.2 %collective-permute-start = (bf16[32,128,128]{2,1,0:T(8,128)(2,1)S(1)}, bf16[32,128,128]{2,1,0:T(8,128)(2,1)S(1)}, u32[]{:S(2)}, u32[]{:S(2)}) collective-permute-start(bf16[32,128,128]{2,1,0:T(8,128)(2,1)S(1)} %bitcast.8), channel_id=1, source_target_pairs={{0,64},{64,128},{128,192},{192,0},{1,65},{65,129},{129,193},{193,1... | collective-permute-start | bytes 3145736 | tf_op jit(solution)/shard_map/ppermute | solution.py:206
  13.0 45.8 %collective-permute-start.1 = (bf16[32,128,128]{2,1,0:T(8,128)(2,1)S(1)}, bf16[32,128,128]{2,1,0:T(8,128)(2,1)S(1)}, u32[]{:S(2)}, u32[]{:S(2)}) collective-permute-start(bf16[32,128,128]{2,1,0:T(8,128)(2,1)S(1)} %bitcast.9), channel_id=1, source_target_pairs={{0,128},{64,192},{128,0},{192,64},{1,129},{65,193},{129,1},{193,65... | collective-permute-start | bytes 3145736 | tf_op jit(solution)/shard_map/ppermute | solution.py:206
  13.6 47.0 %collective-permute-start.2 = (bf16[32,128,128]{2,1,0:T(8,128)(2,1)S(1)}, bf16[32,128,128]{2,1,0:T(8,128)(2,1)S(1)}, u32[]{:S(2)}, u32[]{:S(2)}) collective-permute-start(bf16[32,128,128]{2,1,0:T(8,128)(2,1)S(1)} %bitcast.10), channel_id=1, source_target_pairs={{0,192},{64,0},{128,64},{192,128},{1,193},{65,1},{129,65},{193,129... | collective-permute-start | bytes 3145736 | tf_op jit(solution)/shard_map/ppermute | solution.py:206
  62.9 7.5 %collective-permute-start.3 = (bf16[128,128,128]{2,1,0:T(8,128)(2,1)}, bf16[128,128,128]{2,1,0:T(8,128)(2,1)}, u32[]{:S(2)}, u32[]{:S(2)}) collective-permute-start(bf16[128,128,128]{2,1,0:T(8,128)(2,1)} %pad_maximum_fusion.same_core), channel_id=1, source_target_pairs={{0,32},{32,0},{1,33},{33,1},{2,34},{34,2},{3,35},{35,3},{4,36},{36... | collective-permute-start | bytes 12582920 | tf_op jit(solution)/shard_map/ppermute | solution.py:208
